TPU v7x, 128 devices: a whole 4x4x4 slice. The times are simulated.
128 devices in a mesh: cp: 8 (over x_hi, y), grp: 16 (over z, x_lo, core).
Axes of the slice: x: 4 (x_hi: 2, x_lo: 2; x = x_hi * 2 + x_lo), y: 4, z: 4, core: 2. Of those that a mesh axis runs over, the one named last changes fastest.
Arguments:
- queries: bfloat16 [32, 1024, 2048], P('grp', 'cp'), may hold values from -108 to 108
- keys: bfloat16 [32, 1024, 2048], P('grp', 'cp'), may hold values from -4 to 4
- values: bfloat16 [32, 1024, 2048], P('grp', 'cp'), may hold values from -6 to 6
- lengths: int32 [32], P('grp'), may hold values from 256 to 1024
- frame_map: bfloat16 [2048, 2176], replicated, may hold values from -0.125 to 0.125
- proj_weight: bfloat16 [2176, 4096], P('grp', 'cp'), may hold values from -0.125 to 0.125
- head_weight: bfloat16 [4096, 256], P('cp'), may hold values from -0.375 to 0.375
- act_embed: float32 [7, 4096], P(None, 'cp'), may hold values from -0.5 to 0.5
- actions: int32 [32, 7], P('grp'), may hold values from 0 to 255
- action_mask: int32 [32, 7], P('grp'), may hold values 0 or 1
- group_ids: int32 [32], P('grp'), may hold values from 0 to 3
- rewards: float32 [32], P('grp'), may hold values from -6 to 6
Outputs:
- logprobs: float32 [32, 7], P('grp')
- grad_proj: bfloat16 [2176, 4096], P('grp', 'cp')
- grad_head: bfloat16 [4096, 256], P('cp')
All inputs are finite; a program needn't handle non-finite values. No bound on the sum of `action_mask` on one device may be relied on, other than what follows from the above.
Results may differ from a plain program's by a relative error of at most 0.018.
Values may be sent and summed in bfloat16 or wider, within the bound.
No kernel may reach another device: no remote copies, remote signals or barrier semaphores. Data moves between devices by JAX's collectives and lax.ppermute only.
A program may use at most 128 MiB of HBM per device.

v0:
```python
import math
import jax
import jax.numpy as jnp
from jax import lax
from jax.sharding import PartitionSpec as P

HD = 128
SQRT_HALF = 0.7071067811865476
INV_ROOT_TAU = 0.3989422804014327
NEG_LARGE = -1e30


def in_order(parts, dim):
    parts = jnp.moveaxis(parts, 0, dim)
    shape = parts.shape
    return parts.reshape(*shape[:dim], shape[dim] * shape[dim + 1], *shape[dim + 2 :])


def copy_for_each(array, axis):
    copies = jnp.broadcast_to(array, (lax.axis_size(axis), *array.shape))
    return lax.all_to_all(copies, axis, split_axis=0, concat_axis=0, tiled=True)


def gathered_copies(array, axis, dim):
    return in_order(copy_for_each(array, axis), dim)


def taken_together(array, axis):
    return copy_for_each(array, axis).sum(axis=0)


def together(arrays, axis):
    ravelled, at, outs = (jnp.concatenate([a.reshape(-1) for a in arrays]), 0, [])
    subtotal = taken_together(ravelled, axis)
    for a in arrays:
        outs.append(subtotal[at : at + a.size].reshape(a.shape))
        at += a.size
    return tuple(outs)


def total_of_pieces(array, axis):
    parts = lax.all_gather(array, axis).astype(jnp.float32)
    return parts.sum(axis=0)


def cut_along(array, dim, count):
    before, after = (array.shape[:dim], array.shape[dim + 1 :])
    return jnp.moveaxis(array.reshape(*before, count, -1, *after), dim, 0)


def sent_and_summed(array, axis, dim):
    count = lax.axis_size(axis)
    parts = lax.all_to_all(cut_along(array, dim, count), axis, 0, 0, tiled=True)
    return jnp.sum(parts.astype(jnp.float32), axis=0)


def gelu_exact(values_in):
    return 0.5 * values_in * (1.0 + lax.erf(values_in * SQRT_HALF))


def gelu_slope(values_in):
    return (
        0.5 * (1.0 + lax.erf(values_in * SQRT_HALF))
        + values_in * jnp.exp(-0.5 * values_in * values_in) * INV_ROOT_TAU
    )


def fetch_columns(proj_weight):
    return gathered_copies(proj_weight, "grp", 0)


def attention(queries, keys, values, lengths):
    episodes_here, tokens_here, att_width = queries.shape
    head_count = att_width // HD
    query_heads = queries.reshape(episodes_here, tokens_here, head_count, HD)
    key_heads = keys.reshape(episodes_here, tokens_here, head_count, HD)
    value_heads = values.reshape(episodes_here, tokens_here, head_count, HD)
    query_all, key_all, value_all = (
        lax.all_to_all(query_heads, "cp", split_axis=2, concat_axis=1, tiled=True),
        lax.all_to_all(key_heads, "cp", split_axis=2, concat_axis=1, tiled=True),
        lax.all_to_all(value_heads, "cp", split_axis=2, concat_axis=1, tiled=True),
    )
    seq_span = query_all.shape[1]
    scores = jnp.einsum(
        "eihd,ejhd->ehij", query_all, key_all, preferred_element_type=jnp.float32
    ) / math.sqrt(HD)
    live_keys = (jnp.arange(seq_span, dtype=jnp.int32)[None, :] < lengths[:, None])[
        :, None, None, :
    ]
    scores = jnp.where(live_keys, scores, NEG_LARGE)
    row_max = jnp.max(scores, axis=-1, keepdims=True)
    probs = jnp.where(live_keys, jnp.exp(scores - row_max), 0.0)
    row_total = jnp.sum(probs, axis=-1)
    weighted = jnp.einsum(
        "ehij,ejhd->eihd", probs.astype(jnp.bfloat16), value_all, preferred_element_type=jnp.float32
    )
    output = (weighted / jnp.transpose(row_total, (0, 2, 1))[..., None]).astype(jnp.bfloat16)
    returned = lax.all_to_all(output, "cp", split_axis=1, concat_axis=2, tiled=True)
    return returned.reshape(episodes_here, tokens_here, att_width)


def per_device(
    queries,
    keys,
    values,
    lengths,
    frame_map,
    proj_weight,
    head_weight,
    act_embed,
    actions,
    action_mask,
    group_ids,
    rewards,
):
    episodes_here, tokens_here, att_width = queries.shape
    action_count = act_embed.shape[0]
    lengths_real = lengths.astype(jnp.float32)
    attended = attention(queries, keys, values, lengths)
    proj_cols = fetch_columns(proj_weight)
    frames = jnp.dot(
        attended.reshape(episodes_here * tokens_here, att_width),
        frame_map,
        preferred_element_type=jnp.float32,
    )
    frames = frames.astype(jnp.bfloat16).reshape(episodes_here, tokens_here, frame_map.shape[1])
    all_frames = lax.all_gather(frames, "cp", axis=1, tiled=True)
    seq_span = all_frames.shape[1]
    flat_frames = all_frames.reshape(episodes_here * seq_span, all_frames.shape[2])
    col_count = proj_cols.shape[1]
    pre_act = jnp.dot(flat_frames, proj_cols, preferred_element_type=jnp.float32).reshape(
        episodes_here, seq_span, col_count
    )
    hidden = gelu_exact(pre_act)
    token_mask = (jnp.arange(seq_span, dtype=jnp.int32)[None, :] < lengths[:, None]).astype(
        jnp.float32
    )
    pooled = jnp.sum(token_mask[:, :, None] * hidden, axis=1) / lengths_real[:, None]
    sum_input = pooled[:, None, :] + act_embed[None, :, :]
    head_input = sum_input.astype(jnp.bfloat16).reshape(episodes_here * action_count, col_count)
    partial_logits = jnp.dot(head_input, head_weight, preferred_element_type=jnp.float32)
    episodes_total = episodes_here * lax.axis_size("grp")
    group_count = max(1, episodes_total // 8)
    membership = (group_ids[:, None] == jnp.arange(group_count, dtype=jnp.int32)[None, :]).astype(
        jnp.float32
    )
    masked = action_mask.astype(jnp.float32)
    logits = taken_together(partial_logits, "cp")
    reward_sums, squares, group_sizes, mask_total = together(
        (
            jnp.sum(membership * rewards[:, None], axis=0),
            jnp.sum(membership * (rewards * rewards)[:, None], axis=0),
            jnp.sum(membership, axis=0),
            jnp.sum(masked),
        ),
        "grp",
    )
    log_all = jax.nn.log_softmax(logits, axis=-1)
    bin_ids = jnp.arange(head_weight.shape[1], dtype=jnp.int32)
    picked = (actions.reshape(-1)[:, None] == bin_ids[None, :]).astype(jnp.float32)
    logprobs = jnp.sum(picked * log_all, axis=-1).reshape(episodes_here, action_count)
    size_floor = jnp.maximum(group_sizes, 1.0)
    group_mean = reward_sums / size_floor
    variance = squares / size_floor - group_mean * group_mean
    group_scale = jnp.sqrt(jnp.maximum(variance, 1.0))
    advantage = (rewards - jnp.sum(membership * group_mean[None, :], axis=1)) / jnp.sum(
        membership * group_scale[None, :], axis=1
    )
    loss_weight = (-masked * advantage[:, None] / jnp.maximum(mask_total, 1.0)).reshape(-1)
    logit_grad = (loss_weight[:, None] * (picked - jnp.exp(log_all))).astype(jnp.bfloat16)
    head_term = lax.dot_general(
        head_input, logit_grad, (((0,), (0,)), ((), ())), preferred_element_type=jnp.float32
    )
    grad_head = (
        total_of_pieces(head_term.astype(jnp.bfloat16), "grp")
        .astype(jnp.float32)
        .astype(jnp.bfloat16)
    )
    pull_back = lax.dot_general(
        logit_grad, head_weight, (((1,), (1,)), ((), ())), preferred_element_type=jnp.float32
    )
    pool_grad = jnp.sum(pull_back.reshape(episodes_here, action_count, col_count), axis=1)
    scaled_mask = token_mask / lengths_real[:, None]
    act_grad = (scaled_mask[:, :, None] * pool_grad[:, None, :] * gelu_slope(pre_act)).astype(
        jnp.bfloat16
    )
    act_flat = act_grad.reshape(episodes_here * seq_span, col_count)
    grad_proj = sent_and_summed(
        lax.dot_general(
            flat_frames, act_flat, (((0,), (0,)), ((), ())), preferred_element_type=jnp.float32
        ).astype(jnp.bfloat16),
        "grp",
        0,
    ).astype(jnp.bfloat16)
    return (logprobs, grad_proj, grad_head)


def solution(mesh):
    in_specs = (
        P("grp", "cp", None),
        P("grp", "cp", None),
        P("grp", "cp", None),
        P("grp"),
        P(),
        P("grp", "cp"),
        P("cp", None),
        P(None, "cp"),
        P("grp", None),
        P("grp", None),
        P("grp"),
        P("grp"),
    )
    out_specs = (P("grp", None), P("grp", "cp"), P("cp", None))
    return jax.shard_map(
        per_device, mesh=mesh, in_specs=in_specs, out_specs=out_specs, check_vma=False
    )
```

profile of v0, /device:TPU:1, one launch (start us, length us, event | category | flops | bytes accessed | tf_op | source)
XLA Modules:
  0.0 328.7 jit_solution(10078888517784571058)
XLA Ops:
  7.2 1.7 copy.85
  10.0 7.5 %all-to-all-start = ((bf16[2,128,16,128]{1,3,0,2:T(8,128)(2,1)}), bf16[2,128,16,128]{1,3,0,2:T(8,128)(2,1)S(1)}, u32[]{:S(2)}, u32[]{:S(2)}) async-start(bf16[2,128,16,128]{1,3,0,2:T(8,128)(2,1)} %copy.86), calls=%async_computation | async-start | bytes 2097152 | tf_op jit(solution)/shard_map/all_to_all | solution.py:79
  19.2 12.5 %all-to-all-done = bf16[2,128,16,128]{1,3,0,2:T(8,128)(2,1)S(1)} async-done(((bf16[2,128,16,128]{1,3,0,2:T(8,128)(2,1)}), bf16[2,128,16,128]{1,3,0,2:T(8,128)(2,1)S(1)}, u32[]{:S(2)}, u32[]{:S(2)}) %all-to-all-start) | async-done | bytes 1048608 | tf_op jit(solution)/shard_map/all_to_all | solution.py:79
  31.7 5.9 %all-to-all-start.1 = ((bf16[2,128,16,128]{1,3,0,2:T(8,128)(2,1)}), bf16[2,128,16,128]{1,3,0,2:T(8,128)(2,1)S(1)}, u32[]{:S(2)}, u32[]{:S(2)}) async-start(bf16[2,128,16,128]{1,3,0,2:T(8,128)(2,1)} %copy.90), calls=%async_computation.1 | async-start | bytes 2097152 | tf_op jit(solution)/shard_map/all_to_all | solution.py:80
  37.6 1.6 copy.93
  40.2 11.7 %all-to-all-done.1 = bf16[2,128,16,128]{1,3,0,2:T(8,128)(2,1)S(1)} async-done(((bf16[2,128,16,128]{1,3,0,2:T(8,128)(2,1)}), bf16[2,128,16,128]{1,3,0,2:T(8,128)(2,1)S(1)}, u32[]{:S(2)}, u32[]{:S(2)}) %all-to-all-start.1) | async-done | bytes 1048608 | tf_op jit(solution)/shard_map/all_to_all | solution.py:80
  52.0 5.7 %all-to-all-start.2 = ((bf16[2,128,16,128]{1,3,0,2:T(8,128)(2,1)}), bf16[2,128,16,128]{1,3,0,2:T(8,128)(2,1)S(1)}, u32[]{:S(2)}, u32[]{:S(2)}) async-start(bf16[2,128,16,128]{1,3,0,2:T(8,128)(2,1)} %copy.94), calls=%async_computation.2 | async-start | bytes 2097152 | tf_op jit(solution)/shard_map/all_to_all | solution.py:81
  60.5 11.6 %all-to-all-done.2 = bf16[2,128,16,128]{1,3,0,2:T(8,128)(2,1)S(1)} async-done(((bf16[2,128,16,128]{1,3,0,2:T(8,128)(2,1)}), bf16[2,128,16,128]{1,3,0,2:T(8,128)(2,1)S(1)}, u32[]{:S(2)}, u32[]{:S(2)}) %all-to-all-start.2) | async-done | bytes 1048608 | tf_op jit(solution)/shard_map/all_to_all | solution.py:81
  72.8 11.3 %fusion.32 = (f32[2,2,1024]{2,1,0:T(2,128)S(1)}, bf16[2,2,1024,1024]{2,3,1,0:T(8,128)(2,1)}) fusion(pred[2,1024]{1,0:T(4,128)(4,1)S(1)} %get-tuple-element.11, bf16[2,1024,2,128]{3,1,2,0:T(8,128)(2,1)S(1)} %bitcast.63, bf16[2,1024,2,128]{3,1,2,0:T(8,128)(2,1)} %bitcast.64), kind=kOutput, calls=%fused_computation.59 | convolution fusion | flops 1098908672 | bytes 10504192 | tf_op jit(solution)/shard_map/sub | solution.py:92
  84.0 6.3 %fusion.15 = bf16[2,1024,2,128]{3,1,2,0:T(8,128)(2,1)S(1)} fusion(bf16[2,1024,2,128]{3,1,2,0:T(8,128)(2,1)S(1)} %bitcast.65, bf16[2,2,1024,1024]{2,3,1,0:T(8,128)(2,1)} %get-tuple-element.13, f32[2,1024,2]{1,2,0:T(2,128)S(1)} %bitcast.66), kind=kOutput, calls=%fused_computation.22 | convolution fusion | flops 1074790400 | bytes 10502144 | tf_op jit(solution)/shard_map/ehij,ejhd->eihd/dot_general | solution.py:94
  91.5 21.2 %all_to_all.90 = bf16[2,1024,2,128]{3,2,0,1:T(2,128)(2,1)S(1)} all-to-all(bf16[2,1024,2,128]{3,2,0,1:T(2,128)(2,1)S(1)} %copy.98), channel_id=1, replica_groups=mesh['cp'=8,'grp'=16] {'cp'}, dimensions={1} | all-to-all | bytes 2097152 | tf_op jit(solution)/shard_map/all_to_all | solution.py:98
  114.2 7.2 %convolution_convert_fusion = bf16[256,2176]{1,0:T(8,128)(2,1)} fusion(bf16[256,2048]{1,0:T(8,128)(2,1)S(1)} %reshape_reshape.3, bf16[2048,2176]{1,0:T(8,128)(2,1)} %param.16), kind=kOutput, calls=%fused_computation.20 | convolution fusion | flops 2282258432 | bytes 11075584 | tf_op jit(solution)/shard_map/dot_general | solution.py:121
  122.9 13.2 %all_to_all.91 = f32[16,1,13]{2,1,0:T(1,128)S(1)} all-to-all(f32[16,1,13]{2,1,0:T(1,128)S(1)} %broadcast_in_dim.33), channel_id=1, replica_groups=mesh['cp'=8,'grp'=16] {'grp'}, dimensions={0} | all-to-all | bytes 1664 | tf_op jit(solution)/shard_map/all_to_all | solution.py:21
  136.1 1.6 broadcast_in_dim.31
  137.6 4.2 %all-to-all-start.4 = ((bf16[16,136,512]{2,1,0:T(8,128)(2,1)}), bf16[16,136,512]{2,1,0:T(8,128)(2,1)S(1)}, u32[]{:S(2)}, u32[]{:S(2)}) async-start(bf16[16,136,512]{2,1,0:T(8,128)(2,1)} %broadcast_in_dim.31), calls=%async_computation.4 | async-start | bytes 4456448 | tf_op jit(solution)/shard_map/all_to_all | solution.py:21
  143.5 30.1 %all-to-all-done.4 = bf16[16,136,512]{2,1,0:T(8,128)(2,1)S(1)} async-done(((bf16[16,136,512]{2,1,0:T(8,128)(2,1)}), bf16[16,136,512]{2,1,0:T(8,128)(2,1)S(1)}, u32[]{:S(2)}, u32[]{:S(2)}) %all-to-all-start.4) | async-done | bytes 2228256 | tf_op jit(solution)/shard_map/all_to_all | solution.py:21
  173.6 63.3 %all-gather.4.cloned.1.call-done = bf16[2,1024,2176]{2,1,0:T(8,128)(2,1)} async-done(((bf16[2,128,2176]{2,1,0:T(8,128)(2,1)}), bf16[2,1024,2176]{2,1,0:T(8,128)(2,1)}) %all-gather.4.cloned.1.call-update) | async-done | bytes 8912912 | tf_op jit(solution)/shard_map/all_gather | solution.py:127
  236.9 9.1 %multiply_reduce_fusion = (f32[2,512]{1,0:T(2,128)S(1)}, f32[2,1024,512]{2,1,0:T(8,128)}) fusion(f32[2,1024]{1,0:T(2,128)S(1)} %get-tuple-element.10, bf16[2,1024,2176]{2,1,0:T(8,128)(2,1)} %all-gather.4.cloned.1.call-done, bf16[2176,512,1]{1,0,2:T(8,128)(2,1)S(1)} %bitcast.60), kind=kOutput, calls=%fused_computation.18 | convolution fusion | flops 4569693184 | bytes 15347712 | tf_op jit(solution)/shard_map/dot_general | solution.py:131
  247.0 3.4 %all-to-all-start.5 = ((f32[8,14,256]{2,1,0:T(8,128)}), f32[8,14,256]{2,1,0:T(8,128)S(1)}, u32[]{:S(2)}, u32[]{:S(2)}) async-start(f32[8,14,256]{2,1,0:T(8,128)} %broadcast_in_dim.32), calls=%async_computation.5 | async-start | bytes 262144 | tf_op jit(solution)/shard_map/all_to_all | solution.py:21
  250.5 6.7 %all-to-all-done.5 = f32[8,14,256]{2,1,0:T(8,128)S(1)} async-done(((f32[8,14,256]{2,1,0:T(8,128)}), f32[8,14,256]{2,1,0:T(8,128)S(1)}, u32[]{:S(2)}, u32[]{:S(2)}) %all-to-all-start.5) | async-done | bytes 114720 | tf_op jit(solution)/shard_map/all_to_all | solution.py:21
  258.9 11.9 %fusion.7 = bf16[2176,512]{1,0:T(8,128)(2,1)} fusion(bf16[2,1024,2176]{2,1,0:T(8,128)(2,1)} %all-gather.4.cloned.1.call-done, f32[2,1024,512]{2,1,0:T(8,128)} %get-tuple-element.15, f32[2,512]{1,0:T(2,128)S(1)} %reduce_sum.154, f32[2,1024]{1,0:T(2,128)S(1)} %broadcast_divide_fusion), kind=kOutput, calls=%fused_computation.11 | convolution fusion | flops 4576051200 | bytes 15347712 | tf_op jit(solution)/shard_map/dot_general | solution.py:189
  270.8 6.8 %all-to-all-start.7 = ((bf16[16,136,512]{2,1,0:T(8,128)(2,1)}), bf16[16,136,512]{2,1,0:T(8,128)(2,1)S(1)}, u32[]{:S(2)}, u32[]{:S(2)}) async-start(bf16[16,136,512]{2,1,0:T(8,128)(2,1)} %bitcast.61), calls=%async_computation.7 | async-start | bytes 4456448 | tf_op jit(solution)/shard_map/all_to_all | solution.py:53
  278.4 38.9 %all-to-all-done.7 = bf16[16,136,512]{2,1,0:T(8,128)(2,1)S(1)} async-done(((bf16[16,136,512]{2,1,0:T(8,128)(2,1)}), bf16[16,136,512]{2,1,0:T(8,128)(2,1)S(1)}, u32[]{:S(2)}, u32[]{:S(2)}) %all-to-all-start.7) | async-done | bytes 2228256 | tf_op jit(solution)/shard_map/all_to_all | solution.py:53
  318.3 3.5 %reduce_sum.156 = bf16[512,256]{1,0:T(8,128)(2,1)} reduce(bf16[16,512,256]{2,1,0:T(8,128)(2,1)} %bitcast.51, bf16[]{:T(256)} %constant.36.clone.1), dimensions={0}, to_apply=%region_16.17 | reduce | flops 1966080 | bytes 4456450 | tf_op jit(solution)/shard_map/reduce_sum | solution.py:43
  (67 shorter events, 17.0 us)
Async XLA Ops:
  7.2 239.0 %copy-start = (bf16[512,256]{1,0:T(8,128)(2,1)S(1)}, bf16[512,256]{1,0:T(8,128)(2,1)}, u32[]{:S(2)}) copy-start(bf16[512,256]{1,0:T(8,128)(2,1)} %param.18) | copy-start | bytes 786436
  7.2 10.3 %copy-start.1 = (bf16[2,128,2048]{2,1,0:T(8,128)(2,1)S(1)}, bf16[2,128,2048]{2,1,0:T(8,128)(2,1)}, u32[]{:S(2)}) copy-start(bf16[2,128,2048]{2,1,0:T(8,128)(2,1)} %param.13) | copy-start | bytes 3145732
  10.0 21.7 %all-to-all-start = ((bf16[2,128,16,128]{1,3,0,2:T(8,128)(2,1)}), bf16[2,128,16,128]{1,3,0,2:T(8,128)(2,1)S(1)}, u32[]{:S(2)}, u32[]{:S(2)}) async-start(bf16[2,128,16,128]{1,3,0,2:T(8,128)(2,1)} %copy.86), calls=%async_computation | async-start | bytes 2097152 | tf_op jit(solution)/shard_map/all_to_all | solution.py:79
  19.2 38.5 %copy-start.5 = (s32[2]{0:T(128)S(1)}, s32[2]{0:T(128)}, u32[]{:S(2)}) copy-start(s32[2]{0:T(128)} %param.15) | copy-start | bytes 28
  31.7 20.3 %all-to-all-start.1 = ((bf16[2,128,16,128]{1,3,0,2:T(8,128)(2,1)}), bf16[2,128,16,128]{1,3,0,2:T(8,128)(2,1)S(1)}, u32[]{:S(2)}, u32[]{:S(2)}) async-start(bf16[2,128,16,128]{1,3,0,2:T(8,128)(2,1)} %copy.90), calls=%async_computation.1 | async-start | bytes 2097152 | tf_op jit(solution)/shard_map/all_to_all | solution.py:80
  52.0 20.1 %all-to-all-start.2 = ((bf16[2,128,16,128]{1,3,0,2:T(8,128)(2,1)}), bf16[2,128,16,128]{1,3,0,2:T(8,128)(2,1)S(1)}, u32[]{:S(2)}, u32[]{:S(2)}) async-start(bf16[2,128,16,128]{1,3,0,2:T(8,128)(2,1)} %copy.94), calls=%async_computation.2 | async-start | bytes 2097152 | tf_op jit(solution)/shard_map/all_to_all | solution.py:81
  57.7 179.2 %all-gather.4.cloned.1.call-start = ((), (), s32[]{:S(2)}) async-start(), calls=%async_computation.8 | async-start | bytes 10027008 | tf_op jit(solution)/shard_map/all_gather | solution.py:127
  59.1 13.6 %copy-start.2 = (bf16[2,8,128,2,128]{4,2,1,3,0:T(8,128)(2,1)S(1)}, bf16[2,8,128,2,128]{4,2,1,3,0:T(8,128)(2,1)}, u32[]{:S(2)}) copy-start(bf16[2,8,128,2,128]{4,2,1,3,0:T(8,128)(2,1)} %copy.88) | copy-start | bytes 3145732
  114.2 7.3 %copy-start.7 = (f32[2]{0:T(128)S(1)}, f32[2]{0:T(128)}, u32[]{:S(2)}) copy-start(f32[2]{0:T(128)} %param.23) | copy-start | bytes 28
  114.2 7.3 %copy-start.8 = (s32[2,7]{1,0:T(2,128)S(1)}, s32[2,7]{1,0:T(2,128)}, u32[]{:S(2)}) copy-start(s32[2,7]{1,0:T(2,128)} %param.21) | copy-start | bytes 172
  114.2 7.9 %copy-start.6 = (s32[2]{0:T(128)S(1)}, s32[2]{0:T(128)}, u32[]{:S(2)}) copy-start(s32[2]{0:T(128)} %param.22) | copy-start | bytes 28
  114.2 21.9 %copy-start.3 = (bf16[136,512]{1,0:T(8,128)(2,1)S(1)}, bf16[136,512]{1,0:T(8,128)(2,1)}, u32[]{:S(2)}) copy-start(bf16[136,512]{1,0:T(8,128)(2,1)} %param.17) | copy-start | bytes 417796
  121.4 20.4 %copy-start.9 = (s32[2,7]{1,0:T(2,128)S(1)}, s32[2,7]{1,0:T(2,128)}, u32[]{:S(2)}) copy-start(s32[2,7]{1,0:T(2,128)} %param.20) | copy-start | bytes 172
  137.6 36.0 %all-to-all-start.4 = ((bf16[16,136,512]{2,1,0:T(8,128)(2,1)}), bf16[16,136,512]{2,1,0:T(8,128)(2,1)S(1)}, u32[]{:S(2)}, u32[]{:S(2)}) async-start(bf16[16,136,512]{2,1,0:T(8,128)(2,1)} %broadcast_in_dim.31), calls=%async_computation.4 | async-start | bytes 4456448 | tf_op jit(solution)/shard_map/all_to_all | solution.py:21
  236.9 9.2 %copy-start.4 = (f32[7,512]{1,0:T(8,128)S(1)}, f32[7,512]{1,0:T(8,128)}, u32[]{:S(2)}) copy-start(f32[7,512]{1,0:T(8,128)} %param.19) | copy-start | bytes 43012
  247.0 10.3 %all-to-all-start.5 = ((f32[8,14,256]{2,1,0:T(8,128)}), f32[8,14,256]{2,1,0:T(8,128)S(1)}, u32[]{:S(2)}, u32[]{:S(2)}) async-start(f32[8,14,256]{2,1,0:T(8,128)} %broadcast_in_dim.32), calls=%async_computation.5 | async-start | bytes 262144 | tf_op jit(solution)/shard_map/all_to_all | solution.py:21
  250.3 67.9 %all-gather.6.cloned.1.call-start = ((), (), s32[]{:S(2)}) async-start(), calls=%async_computation.9 | async-start | bytes 4456448 | tf_op jit(solution)/shard_map/all_gather | solution.py:42
  270.8 46.5 %all-to-all-start.7 = ((bf16[16,136,512]{2,1,0:T(8,128)(2,1)}), bf16[16,136,512]{2,1,0:T(8,128)(2,1)S(1)}, u32[]{:S(2)}, u32[]{:S(2)}) async-start(bf16[16,136,512]{2,1,0:T(8,128)(2,1)} %bitcast.61), calls=%async_computation.7 | async-start | bytes 4456448 | tf_op jit(solution)/shard_map/all_to_all | solution.py:53
Sparse Core Ops, SparseCore 0:
  121.5 115.2 all-gather.3
  258.7 59.1 all-gather.5
where the time goes:
time: 329 us
  waiting for transfers between devices  175 us (53%)
  matrix products  47.1 us (14%)
  blocking collectives  34.3 us (10%)
  starting transfers between devices  33.5 us (10%)
  local copies, waits for them, and re-layouts  16.9 us (5%)
  between operations  14.9 us (5%)
  other arithmetic  7.1 us (2%)
    all_gather x1, waiting for transfers between devices, per_device(): all_frames = lax.all_gather(frames, 'cp', axis=1, tiled=True)  63.3 us
    all_to_all x1, waiting for transfers between devices, sent_and_summed(): parts = lax.all_to_all(cut_along(array, dim, count), axis, 0, 0, tiled=True)  38.9 us
    all_to_all x2, waiting for transfers between devices, copy_for_each(): return lax.all_to_all(copies, axis, split_axis=0, concat_axis=0, tiled=True)  36.8 us
    all_to_all x1, blocking collectives, attention(): lax.all_to_all(output, 'cp', split_axis=1, concat_axis=2, tiled=True)  21.2 us
    all_to_all x1, blocking collectives, copy_for_each(): return lax.all_to_all(copies, axis, split_axis=0, concat_axis=0, tiled=True)  13.2 us
    all_to_all x1, waiting for transfers between devices, attention(): lax.all_to_all(query_heads, 'cp', split_axis=2, concat_axis=1, tiled=True)  12.5 us
    dot_general x1, matrix products, per_device(): lax.dot_general(flat_frames, act_flat, (((0,), (0,)), ((), ())), preferre...  11.9 us
    all_to_all x1, waiting for transfers between devices, attention(): lax.all_to_all(key_heads, 'cp', split_axis=2, concat_axis=1, tiled=True)  11.7 us
  transfers between devices with their start and end apart: 8, of which 7 were waited for; matrix products, arithmetic and copies ran while one was open for 8% of the time, Pallas kernels for 0%

commit v1 on v0

--- a/solution.py
+++ b/solution.py
@@ -124,7 +124,13 @@
         preferred_element_type=jnp.float32,
     )
     frames = frames.astype(jnp.bfloat16).reshape(episodes_here, tokens_here, frame_map.shape[1])
-    all_frames = lax.all_gather(frames, "cp", axis=1, tiled=True)
+
+    def choose_ranges(here_x):
+        return jnp.concatenate(
+            lax.all_to_all(jnp.stack([here_x for _ in range(lax.psum(1, "cp"))]), "cp", 0, 0), 1
+        )
+
+    all_frames = choose_ranges(frames)
     seq_span = all_frames.shape[1]
     flat_frames = all_frames.reshape(episodes_here * seq_span, all_frames.shape[2])
     col_count = proj_cols.shape[1]

time: 329 us -> 364 us (1.11)
  blocking collectives: 34.3 us -> 105 us
  waiting for transfers between devices: 175 us -> 112 us
  starting transfers between devices: 33.5 us -> 48.3 us
  local copies, waits for them, and re-layouts: 16.9 us -> 27.6 us
  other arithmetic: 7.1 us -> 11.1 us
    all_to_all x2 -> x1, blocking collectives: 34.3 us -> 105 us  [choose_ranges(): lax.all_to_all(jnp.stack([here_x for _ in range(lax.psum(1, 'cp'))]), 'cp...]
    all_gather x1 -> x0, waiting for transfers between devices: 63.3 us -> none  [per_device(): all_frames = lax.all_gather(frames, 'cp', axis=1, tiled=True)]
    all_to_all x0 -> x1, waiting for transfers between devices: none -> 13 us  [attention(): lax.all_to_all(output, 'cp', split_axis=1, concat_axis=2, tiled=True)]
    all_to_all x2 -> x3, waiting for transfers between devices: 36.8 us -> 25.4 us  [copy_for_each(): return lax.all_to_all(copies, axis, split_axis=0, concat_axis=0, tiled=True)]
    all_to_all x2 -> x3, starting transfers between devices: 7.55 us -> 17.8 us  [copy_for_each(): return lax.all_to_all(copies, axis, split_axis=0, concat_axis=0, tiled=True)]
    all_to_all x0 -> x1, local copies, waits for them, and re-layouts: none -> 7.97 us  [choose_ranges(): lax.all_to_all(jnp.stack([here_x for _ in range(lax.psum(1, 'cp'))]), 'cp...]
    all_to_all x0 -> x1, starting transfers between devices: none -> 5.7 us  [attention(): lax.all_to_all(output, 'cp', split_axis=1, concat_axis=2, tiled=True)]
    convert_element_type x0 -> x1, other arithmetic: none -> 4.01 us  [per_device(): (scaled_mask[:, :, None] * pool_grad[:, None, :] * gelu_slope(pre_act)).a...]
  transfers between devices with their start and end apart: 8 -> 9, of which waited for: 7 -> 7; matrix products, arithmetic and copies ran while one was open for 8% -> 11% of each run, Pallas kernels for 0% -> 0%
where the time goes in v1:
time: 364 us; the launch traced here: 363 us
  waiting for transfers between devices  112 us (31%)
  blocking collectives  105 us (29%)
  starting transfers between devices  48.3 us (13%)
  matrix products  44.1 us (12%)
  local copies, waits for them, and re-layouts  27.6 us (8%)
  between operations  14.9 us (4%)
  other arithmetic  11.1 us (3%)
    all_to_all x1, blocking collectives, choose_ranges(): lax.all_to_all(jnp.stack([here_x for _ in range(lax.psum(1, 'cp'))]), 'cp...  105 us
    all_to_all x1, waiting for transfers between devices, sent_and_summed(): parts = lax.all_to_all(cut_along(array, dim, count), axis, 0, 0, tiled=True)  37.6 us
    all_to_all x3, waiting for transfers between devices, copy_for_each(): return lax.all_to_all(copies, axis, split_axis=0, concat_axis=0, tiled=True)  25.4 us
    all_to_all x3, starting transfers between devices, copy_for_each(): return lax.all_to_all(copies, axis, split_axis=0, concat_axis=0, tiled=True)  17.8 us
    all_to_all x1, waiting for transfers between devices, attention(): lax.all_to_all(output, 'cp', split_axis=1, concat_axis=2, tiled=True)  13 us
    all_to_all x1, waiting for transfers between devices, attention(): lax.all_to_all(value_heads, 'cp', split_axis=2, concat_axis=1, tiled=True)  12.5 us
    all_to_all x1, waiting for transfers between devices, attention(): lax.all_to_all(query_heads, 'cp', split_axis=2, concat_axis=1, tiled=True)  11.7 us
    all_to_all x1, waiting for transfers between devices, attention(): lax.all_to_all(key_heads, 'cp', split_axis=2, concat_axis=1, tiled=True)  11.7 us
  transfers between devices with their start and end apart: 9, of which 7 were waited for; matrix products, arithmetic and copies ran while one was open for 11% of the time, Pallas kernels for 0%

profile of v1, /device:TPU:1, one launch (start us, length us, event | category | flops | bytes accessed | tf_op | source)
XLA Modules:
  0.0 362.6 jit_solution(9954154206239685788)
XLA Ops:
  10.0 7.5 %all-to-all-start.2 = ((bf16[2,128,16,128]{1,3,0,2:T(8,128)(2,1)}), bf16[2,128,16,128]{1,3,0,2:T(8,128)(2,1)S(1)}, u32[]{:S(2)}, u32[]{:S(2)}) async-start(bf16[2,128,16,128]{1,3,0,2:T(8,128)(2,1)} %copy.107), calls=%async_computation.2 | async-start | bytes 2097152 | tf_op jit(solution)/shard_map/all_to_all | solution.py:81
  19.2 12.5 %all-to-all-done.2 = bf16[2,128,16,128]{1,3,0,2:T(8,128)(2,1)S(1)} async-done(((bf16[2,128,16,128]{1,3,0,2:T(8,128)(2,1)}), bf16[2,128,16,128]{1,3,0,2:T(8,128)(2,1)S(1)}, u32[]{:S(2)}, u32[]{:S(2)}) %all-to-all-start.2) | async-done | bytes 1048608 | tf_op jit(solution)/shard_map/all_to_all | solution.py:81
  31.7 5.9 %all-to-all-start = ((bf16[2,128,16,128]{1,3,0,2:T(8,128)(2,1)}), bf16[2,128,16,128]{1,3,0,2:T(8,128)(2,1)S(1)}, u32[]{:S(2)}, u32[]{:S(2)}) async-start(bf16[2,128,16,128]{1,3,0,2:T(8,128)(2,1)} %copy.99), calls=%async_computation | async-start | bytes 2097152 | tf_op jit(solution)/shard_map/all_to_all | solution.py:79
  40.2 11.7 %all-to-all-done = bf16[2,128,16,128]{1,3,0,2:T(8,128)(2,1)S(1)} async-done(((bf16[2,128,16,128]{1,3,0,2:T(8,128)(2,1)}), bf16[2,128,16,128]{1,3,0,2:T(8,128)(2,1)S(1)}, u32[]{:S(2)}, u32[]{:S(2)}) %all-to-all-start) | async-done | bytes 1048608 | tf_op jit(solution)/shard_map/all_to_all | solution.py:79
  52.0 5.7 %all-to-all-start.1 = ((bf16[2,128,16,128]{1,3,0,2:T(8,128)(2,1)}), bf16[2,128,16,128]{1,3,0,2:T(8,128)(2,1)S(1)}, u32[]{:S(2)}, u32[]{:S(2)}) async-start(bf16[2,128,16,128]{1,3,0,2:T(8,128)(2,1)} %copy.103), calls=%async_computation.1 | async-start | bytes 2097152 | tf_op jit(solution)/shard_map/all_to_all | solution.py:80
  60.5 11.7 %all-to-all-done.1 = bf16[2,128,16,128]{1,3,0,2:T(8,128)(2,1)S(1)} async-done(((bf16[2,128,16,128]{1,3,0,2:T(8,128)(2,1)}), bf16[2,128,16,128]{1,3,0,2:T(8,128)(2,1)S(1)}, u32[]{:S(2)}, u32[]{:S(2)}) %all-to-all-start.1) | async-done | bytes 1048608 | tf_op jit(solution)/shard_map/all_to_all | solution.py:80
  72.8 11.3 %fusion.22 = (f32[2,2,1024]{2,1,0:T(2,128)S(1)}, bf16[2,2,1024,1024]{2,3,1,0:T(8,128)(2,1)}) fusion(pred[2,1024]{1,0:T(4,128)(4,1)S(1)} %get-tuple-element.11, bf16[2,1024,2,128]{3,1,2,0:T(8,128)(2,1)} %bitcast.70, bf16[2,1024,2,128]{3,1,2,0:T(8,128)(2,1)S(1)} %bitcast.71), kind=kOutput, calls=%fused_computation.50 | convolution fusion | flops 1098908672 | bytes 10504192 | tf_op jit(solution)/shard_map/sub | solution.py:92
  84.1 6.3 %fusion.13 = bf16[2,1024,2,128]{3,1,2,0:T(8,128)(2,1)S(1)} fusion(bf16[2,1024,2,128]{3,1,2,0:T(8,128)(2,1)S(1)} %bitcast.69, bf16[2,2,1024,1024]{2,3,1,0:T(8,128)(2,1)} %get-tuple-element.13, f32[2,1024,2]{1,2,0:T(2,128)S(1)} %bitcast.72), kind=kOutput, calls=%fused_computation.21 | convolution fusion | flops 1074790400 | bytes 10502144 | tf_op jit(solution)/shard_map/ehij,ejhd->eihd/dot_general | solution.py:94
  92.6 5.7 %all-to-all-start.3 = ((bf16[2,1024,2,128]{3,2,0,1:T(2,128)(2,1)}), bf16[2,1024,2,128]{3,2,0,1:T(2,128)(2,1)S(1)}, u32[]{:S(2)}, u32[]{:S(2)}) async-start(bf16[2,1024,2,128]{3,2,0,1:T(2,128)(2,1)} %copy.111), calls=%async_computation.3 | async-start | bytes 2097152 | tf_op jit(solution)/shard_map/all_to_all | solution.py:98
  99.7 13.0 %all-to-all-done.3 = bf16[2,1024,2,128]{3,2,0,1:T(2,128)(2,1)S(1)} async-done(((bf16[2,1024,2,128]{3,2,0,1:T(2,128)(2,1)}), bf16[2,1024,2,128]{3,2,0,1:T(2,128)(2,1)S(1)}, u32[]{:S(2)}, u32[]{:S(2)}) %all-to-all-start.3) | async-done | bytes 1048608 | tf_op jit(solution)/shard_map/all_to_all | solution.py:98
  113.3 7.6 %all-to-all-start.7 = ((f32[16,1,13]{2,1,0:T(1,128)}), f32[16,1,13]{2,1,0:T(1,128)S(1)}, u32[]{:S(2)}, u32[]{:S(2)}) async-start(f32[16,1,13]{2,1,0:T(1,128)} %broadcast_in_dim.33), calls=%async_computation.7 | async-start | bytes 16384 | tf_op jit(solution)/shard_map/all_to_all | solution.py:21
  122.4 6.1 %convolution_convert_fusion.1 = bf16[256,2176]{1,0:T(8,128)(2,1)S(1)} fusion(bf16[256,2048]{1,0:T(8,128)(2,1)S(1)} %reshape_reshape.6, bf16[2048,2176]{1,0:T(8,128)(2,1)} %param.16), kind=kOutput, calls=%fused_computation.19 | convolution fusion | flops 2282258432 | bytes 11075584 | tf_op jit(solution)/shard_map/dot_general | solution.py:121
  129.7 104.8 %all_to_all.95 = bf16[8,2,128,2176]{3,2,1,0:T(8,128)(2,1)} all-to-all(bf16[8,2,128,2176]{3,2,1,0:T(8,128)(2,1)S(1)} %stack.3), channel_id=1, replica_groups=mesh['cp'=8,'grp'=16] {'cp'}, dimensions={0} | all-to-all | bytes 17825792 | tf_op jit(solution)/shard_map/all_to_all | solution.py:130
  236.1 6.9 %all-to-all-start.5 = ((bf16[16,136,512]{2,1,0:T(8,128)(2,1)}), bf16[16,136,512]{2,1,0:T(8,128)(2,1)S(1)}, u32[]{:S(2)}, u32[]{:S(2)}) async-start(bf16[16,136,512]{2,1,0:T(8,128)(2,1)} %broadcast_in_dim.31), calls=%async_computation.5 | async-start | bytes 4456448 | tf_op jit(solution)/shard_map/all_to_all | solution.py:21
  244.6 8.0 %copy.113 = bf16[8,2,128,2176]{3,2,0,1:T(8,128)(2,1)} copy(bf16[8,2,128,2176]{3,2,1,0:T(8,128)(2,1)} %all_to_all.95) | data formatting | bytes 17825792 | tf_op jit(solution)/shard_map/all_to_all | solution.py:130
  252.6 18.7 %all-to-all-done.5 = bf16[16,136,512]{2,1,0:T(8,128)(2,1)S(1)} async-done(((bf16[16,136,512]{2,1,0:T(8,128)(2,1)}), bf16[16,136,512]{2,1,0:T(8,128)(2,1)S(1)}, u32[]{:S(2)}, u32[]{:S(2)}) %all-to-all-start.5) | async-done | bytes 2228256 | tf_op jit(solution)/shard_map/all_to_all | solution.py:21
  271.3 9.1 %multiply_reduce_fusion = (f32[2,512]{1,0:T(2,128)S(1)}, f32[2,1024,512]{2,1,0:T(8,128)}) fusion(f32[2,1024]{1,0:T(2,128)S(1)} %get-tuple-element.10, bf16[2,1024,2176]{2,1,0:T(8,128)(2,1)} %bitcast.54, bf16[2176,512,1]{1,0,2:T(8,128)(2,1)S(1)} %bitcast.65), kind=kOutput, calls=%fused_computation.17 | convolution fusion | flops 4569693184 | bytes 15347712 | tf_op jit(solution)/shard_map/dot_general | solution.py:137
  281.4 3.4 all-to-all-start.6
  285.0 6.7 %all-to-all-done.6 = f32[8,14,256]{2,1,0:T(8,128)S(1)} async-done(((f32[8,14,256]{2,1,0:T(8,128)}), f32[8,14,256]{2,1,0:T(8,128)S(1)}, u32[]{:S(2)}, u32[]{:S(2)}) %all-to-all-start.6) | async-done | bytes 114720 | tf_op jit(solution)/shard_map/all_to_all | solution.py:21
  293.3 4.0 %fusion.12 = bf16[2,1024,512]{2,1,0:T(8,128)(2,1)S(1)} fusion(f32[2,1024,512]{2,1,0:T(8,128)} %get-tuple-element.15, f32[2,512]{1,0:T(2,128)S(1)} %reduce_sum.154, f32[2,1024]{1,0:T(2,128)S(1)} %broadcast_divide_fusion), kind=kLoop, calls=%fused_computation.16 | loop fusion | flops 11534336 | bytes 6303744 | tf_op jit(solution)/shard_map/convert_element_type | solution.py:190
  297.3 9.8 %convolution_convert_fusion = bf16[2176,512]{1,0:T(8,128)(2,1)} fusion(bf16[2048,2176]{1,0:T(8,128)(2,1)} %bitcast.55, bf16[2048,512]{1,0:T(8,128)(2,1)S(1)} %bitcast.67), kind=kOutput, calls=%fused_computation.10 | convolution fusion | flops 4564516864 | bytes 13238272 | tf_op jit(solution)/shard_map/dot_general | solution.py:195
  307.2 5.6 %all-to-all-start.8 = ((bf16[16,136,512]{2,1,0:T(8,128)(2,1)}), bf16[16,136,512]{2,1,0:T(8,128)(2,1)S(1)}, u32[]{:S(2)}, u32[]{:S(2)}) async-start(bf16[16,136,512]{2,1,0:T(8,128)(2,1)} %bitcast.66), calls=%async_computation.8 | async-start | bytes 4456448 | tf_op jit(solution)/shard_map/all_to_all | solution.py:53
  313.6 37.6 %all-to-all-done.8 = bf16[16,136,512]{2,1,0:T(8,128)(2,1)S(1)} async-done(((bf16[16,136,512]{2,1,0:T(8,128)(2,1)}), bf16[16,136,512]{2,1,0:T(8,128)(2,1)S(1)}, u32[]{:S(2)}, u32[]{:S(2)}) %all-to-all-start.8) | async-done | bytes 2228256 | tf_op jit(solution)/shard_map/all_to_all | solution.py:53
  352.3 3.5 reduce_sum.156
  (70 shorter events, 24.5 us)
Async XLA Ops:
  7.2 273.4 %copy-start = (bf16[512,256]{1,0:T(8,128)(2,1)S(1)}, bf16[512,256]{1,0:T(8,128)(2,1)}, u32[]{:S(2)}) copy-start(bf16[512,256]{1,0:T(8,128)(2,1)} %param.18) | copy-start | bytes 786436
  7.2 10.3 %copy-start.1 = (bf16[2,128,2048]{2,1,0:T(8,128)(2,1)S(1)}, bf16[2,128,2048]{2,1,0:T(8,128)(2,1)}, u32[]{:S(2)}) copy-start(bf16[2,128,2048]{2,1,0:T(8,128)(2,1)} %param.12) | copy-start | bytes 3145732
  10.0 21.7 %all-to-all-start.2 = ((bf16[2,128,16,128]{1,3,0,2:T(8,128)(2,1)}), bf16[2,128,16,128]{1,3,0,2:T(8,128)(2,1)S(1)}, u32[]{:S(2)}, u32[]{:S(2)}) async-start(bf16[2,128,16,128]{1,3,0,2:T(8,128)(2,1)} %copy.107), calls=%async_computation.2 | async-start | bytes 2097152 | tf_op jit(solution)/shard_map/all_to_all | solution.py:81
  19.2 38.5 %copy-start.5 = (s32[2]{0:T(128)S(1)}, s32[2]{0:T(128)}, u32[]{:S(2)}) copy-start(s32[2]{0:T(128)} %param.15) | copy-start | bytes 28
  31.7 20.3 %all-to-all-start = ((bf16[2,128,16,128]{1,3,0,2:T(8,128)(2,1)}), bf16[2,128,16,128]{1,3,0,2:T(8,128)(2,1)S(1)}, u32[]{:S(2)}, u32[]{:S(2)}) async-start(bf16[2,128,16,128]{1,3,0,2:T(8,128)(2,1)} %copy.99), calls=%async_computation | async-start | bytes 2097152 | tf_op jit(solution)/shard_map/all_to_all | solution.py:79
  52.0 20.1 %all-to-all-start.1 = ((bf16[2,128,16,128]{1,3,0,2:T(8,128)(2,1)}), bf16[2,128,16,128]{1,3,0,2:T(8,128)(2,1)S(1)}, u32[]{:S(2)}, u32[]{:S(2)}) async-start(bf16[2,128,16,128]{1,3,0,2:T(8,128)(2,1)} %copy.103), calls=%async_computation.1 | async-start | bytes 2097152 | tf_op jit(solution)/shard_map/all_to_all | solution.py:80
  72.8 11.4 %copy-start.2 = (bf16[2,8,128,2,128]{4,2,1,3,0:T(8,128)(2,1)S(1)}, bf16[2,8,128,2,128]{4,2,1,3,0:T(8,128)(2,1)}, u32[]{:S(2)}) copy-start(bf16[2,8,128,2,128]{4,2,1,3,0:T(8,128)(2,1)} %copy.109) | copy-start | bytes 3145732
  90.5 7.8 %copy-start.7 = (f32[2]{0:T(128)S(1)}, f32[2]{0:T(128)}, u32[]{:S(2)}) copy-start(f32[2]{0:T(128)} %param.23) | copy-start | bytes 28
  90.5 7.8 %copy-start.8 = (s32[2,7]{1,0:T(2,128)S(1)}, s32[2,7]{1,0:T(2,128)}, u32[]{:S(2)}) copy-start(s32[2,7]{1,0:T(2,128)} %param.21) | copy-start | bytes 172
  90.5 8.4 %copy-start.6 = (s32[2]{0:T(128)S(1)}, s32[2]{0:T(128)}, u32[]{:S(2)}) copy-start(s32[2]{0:T(128)} %param.22) | copy-start | bytes 28
  92.6 20.1 %all-to-all-start.3 = ((bf16[2,1024,2,128]{3,2,0,1:T(2,128)(2,1)}), bf16[2,1024,2,128]{3,2,0,1:T(2,128)(2,1)S(1)}, u32[]{:S(2)}, u32[]{:S(2)}) async-start(bf16[2,1024,2,128]{3,2,0,1:T(2,128)(2,1)} %copy.111), calls=%async_computation.3 | async-start | bytes 2097152 | tf_op jit(solution)/shard_map/all_to_all | solution.py:98
  113.3 15.3 %all-to-all-start.7 = ((f32[16,1,13]{2,1,0:T(1,128)}), f32[16,1,13]{2,1,0:T(1,128)S(1)}, u32[]{:S(2)}, u32[]{:S(2)}) async-start(f32[16,1,13]{2,1,0:T(1,128)} %broadcast_in_dim.33), calls=%async_computation.7 | async-start | bytes 16384 | tf_op jit(solution)/shard_map/all_to_all | solution.py:21
  129.7 104.8 %copy-start.3 = (bf16[136,512]{1,0:T(8,128)(2,1)S(1)}, bf16[136,512]{1,0:T(8,128)(2,1)}, u32[]{:S(2)}) copy-start(bf16[136,512]{1,0:T(8,128)(2,1)} %param.17) | copy-start | bytes 417796
  234.5 8.4 %copy-start.9 = (s32[2,7]{1,0:T(2,128)S(1)}, s32[2,7]{1,0:T(2,128)}, u32[]{:S(2)}) copy-start(s32[2,7]{1,0:T(2,128)} %param.20) | copy-start | bytes 172
  236.1 35.3 %all-to-all-start.5 = ((bf16[16,136,512]{2,1,0:T(8,128)(2,1)}), bf16[16,136,512]{2,1,0:T(8,128)(2,1)S(1)}, u32[]{:S(2)}, u32[]{:S(2)}) async-start(bf16[16,136,512]{2,1,0:T(8,128)(2,1)} %broadcast_in_dim.31), calls=%async_computation.5 | async-start | bytes 4456448 | tf_op jit(solution)/shard_map/all_to_all | solution.py:21
  271.3 9.2 %copy-start.4 = (f32[7,512]{1,0:T(8,128)S(1)}, f32[7,512]{1,0:T(8,128)}, u32[]{:S(2)}) copy-start(f32[7,512]{1,0:T(8,128)} %param.19) | copy-start | bytes 43012
  281.4 10.3 %all-to-all-start.6 = ((f32[8,14,256]{2,1,0:T(8,128)}), f32[8,14,256]{2,1,0:T(8,128)S(1)}, u32[]{:S(2)}, u32[]{:S(2)}) async-start(f32[8,14,256]{2,1,0:T(8,128)} %broadcast_in_dim.32), calls=%async_computation.6 | async-start | bytes 262144 | tf_op jit(solution)/shard_map/all_to_all | solution.py:21
  284.8 67.5 %all-gather.3.cloned.1.call-start = ((), (), s32[]{:S(2)}) async-start(), calls=%async_computation.9 | async-start | bytes 4456448 | tf_op jit(solution)/shard_map/all_gather | solution.py:42
  307.2 44.1 %all-to-all-start.8 = ((bf16[16,136,512]{2,1,0:T(8,128)(2,1)}), bf16[16,136,512]{2,1,0:T(8,128)(2,1)S(1)}, u32[]{:S(2)}, u32[]{:S(2)}) async-start(bf16[16,136,512]{2,1,0:T(8,128)(2,1)} %bitcast.66), calls=%async_computation.8 | async-start | bytes 4456448 | tf_op jit(solution)/shard_map/all_to_all | solution.py:53
Sparse Core Ops, SparseCore 0:
  293.1 57.2 all-gather.2
